TPU v7x, 32 devices: a whole 2x2x4 slice. The times are simulated.
32 devices in a mesh: seq: 8 (over z, y), tp: 4 (over x, core).
Axes of the slice: x: 2, y: 2, z: 4, core: 2. Of those that a mesh axis runs over, the one named last changes fastest.
Arguments:
- tokens: bfloat16 [8192, 1152], P('seq', 'tp'), may hold values from -6 to 6
- out_grad: bfloat16 [8192, 1152], P('seq', 'tp'), may hold values from -6 to 6
- route_mask: int32 [8192], P('seq'), may hold values from 0 to 1, as said below
- kept_counts: int32 [32], replicated, may hold values from 64 to 192, as said below
- labels: int32 [32], replicated, may hold values from 0 to 1000
- timesteps: int32 [32], replicated, may hold values from 0 to 999
- class_table: bfloat16 [1001, 1152], replicated, may hold values from -6 to 6
- ada_weight: bfloat16 [1152, 6, 1152], P(None, None, 'tp'), may hold values from -0.1875 to 0.1875
- ada_bias: bfloat16 [6, 1152], P(None, 'tp'), may hold values from -2 to 2
- qkv_weight: bfloat16 [1152, 3, 1152], P(None, None, 'tp'), may hold values from -0.1875 to 0.1875
- qv_bias: bfloat16 [2, 1152], P(None, 'tp'), may hold values from -2 to 2
- proj_weight: bfloat16 [1152, 1152], P('tp'), may hold values from -0.5 to 0.5
- proj_bias: bfloat16 [1152], P('tp'), may hold values from -2 to 2
- hidden_weight: bfloat16 [1152, 4608], P(None, 'tp'), may hold values from -0.1875 to 0.1875
- hidden_bias: bfloat16 [4608], P('tp'), may hold values from -2 to 2
- output_weight: bfloat16 [4608, 1152], P('tp'), may hold values from -0.09375 to 0.09375
- output_bias: bfloat16 [1152], P('tp'), may hold values from -2 to 2
Outputs:
- output: bfloat16 [8192, 1152], P('seq', 'tp')
- tokens_grad: bfloat16 [8192, 1152], P('seq', 'tp')
- class_grad: float32 [1001, 1152], P(None, 'seq')
- ada_weight_grad: float32 [1152, 6, 1152], P('seq', None, 'tp')
- ada_bias_grad: float32 [6, 1152], P(None, 'tp')
- qkv_weight_grad: float32 [1152, 3, 1152], P('seq', None, 'tp')
- qv_bias_grad: float32 [2, 1152], P(None, 'tp')
- proj_weight_grad: float32 [1152, 1152], P('tp', 'seq')
- proj_bias_grad: float32 [1152], P('tp')
- hidden_weight_grad: float32 [1152, 4608], P('seq', 'tp')
- hidden_bias_grad: float32 [4608], P('tp')
- output_weight_grad: float32 [4608, 1152], P('tp', 'seq')
- output_bias_grad: float32 [1152], P('tp')
Inputs may be any that keep to these rules, and one draw needn't show every extreme that they name: route_mask keeps exactly kept_counts[i] of the 256 tokens of image i. The kept tokens of all images number 512 * 8; the kept tokens of the first j * 4 images exceed j * 512 by 0 to 128 for every j, by exactly 128 for some j, and by 0 at the end. Every aligned block of 4 images has one image with 192 kept tokens. `route_mask`: consistent with kept_counts.
All inputs are finite; a program needn't handle non-finite values.
Results may differ from a plain program's by a relative error of at most 0.025.
The roundings to bfloat16 on the way count: a program that leaves them out, or rounds other values in their place, can miss the bound.
Values may be sent and summed in bfloat16 or wider, within the bound.
A program may use at most 192 MiB of HBM per device.

v0:
```python
import math
import jax
import jax.numpy as jnp
from jax import lax
from jax.sharding import PartitionSpec as P

HEAD_DIM = 72
IMG_DEV = 4
ROWS = 640
NORM_EPS = 1e-06
HIGHEST = lax.Precision.HIGHEST


def exact_dot(left_mat, right_mat):
    return jnp.dot(left_mat, right_mat, precision=HIGHEST, preferred_element_type=jnp.float32)


def time_embed(step_ids, model_width):
    half_width = model_width // 2
    frequency = jnp.exp(-math.log(10000.0) * jnp.arange(half_width, dtype=jnp.float32) / half_width)
    angles = step_ids.astype(jnp.float32)[:, None] * frequency[None, :]
    return jnp.concatenate([jnp.cos(angles), jnp.sin(angles)], axis=1)


def norm_rows(values):
    centered = values - jnp.mean(values, axis=1, keepdims=True)
    inverse = lax.rsqrt(jnp.mean(centered * centered, axis=1, keepdims=True) + NORM_EPS)
    return (centered * inverse, inverse)


def gelu_tanh(values):
    return jax.nn.gelu(values, approximate=True)


def local(
    tokens,
    out_grad,
    route_mask,
    kept_counts,
    labels,
    timesteps,
    class_table,
    ada_weight,
    ada_bias,
    qkv_weight,
    qv_bias,
    proj_weight,
    proj_bias,
    hidden_weight,
    hidden_bias,
    output_weight,
    output_bias,
):
    f32, bf16 = (jnp.float32, jnp.bfloat16)
    seq_index = lax.axis_index("seq")
    tp_index = lax.axis_index("tp")
    seq_size = lax.axis_size("seq")
    col_local = tokens.shape[1]
    model_width = class_table.shape[1]
    head_cols = qkv_weight.shape[2]
    heads_local = head_cols // HEAD_DIM
    slice_width = model_width // seq_size
    images = kept_counts.shape[0]
    scale_factor = HEAD_DIM ** (-0.5)
    col_start = tp_index * col_local
    first_image = seq_index * IMG_DEV
    own_counts = lax.dynamic_slice_in_dim(kept_counts, first_image, IMG_DEV)
    own_ends = jnp.cumsum(own_counts)
    rank = jnp.where(route_mask > 0, jnp.cumsum(route_mask) - 1, -1)
    row_ids = jnp.arange(ROWS, dtype=jnp.int32)
    place = (rank[None, :] == row_ids[:, None]).astype(bf16)
    row_image = jnp.sum((own_ends[None, :] <= row_ids[:, None]).astype(jnp.int32), axis=1)
    row_onehot = (row_image[:, None] == jnp.arange(IMG_DEV, dtype=jnp.int32)[None, :]).astype(f32)

    def whole_rows(part_rows):
        return lax.all_gather(part_rows, "tp", axis=1, tiled=True)

    def column_sum(part_rows):
        return lax.psum_scatter(
            part_rows.astype(bf16), "tp", scatter_dimension=1, tiled=True
        ).astype(f32)

    def own_cols(full_rows):
        return lax.dynamic_slice_in_dim(full_rows, col_start, col_local, 1)

    def reinsert(rows_new, initial):
        placed = jnp.einsum("rt,rc->tc", place, rows_new, preferred_element_type=f32).astype(bf16)
        return jnp.where(route_mask[:, None] > 0, placed, initial)

    label_hot = (
        labels[:, None] == jnp.arange(class_table.shape[0], dtype=jnp.int32)[None, :]
    ).astype(bf16)
    condition = jnp.dot(label_hot, class_table, preferred_element_type=f32) + time_embed(
        timesteps, model_width
    )
    cond_low = jax.nn.silu(condition).astype(bf16)
    cond_own = lax.dynamic_slice_in_dim(cond_low, first_image, IMG_DEV)
    mod_own = (
        jnp.einsum("wd,dcf->wcf", cond_own, ada_weight, preferred_element_type=f32)
        + ada_bias.astype(f32)[None]
    )
    mod_full = lax.all_gather(mod_own, "tp", axis=2, tiled=True)

    def row_full(stretch_id):
        return exact_dot(row_onehot, mod_full[:, stretch_id, :])

    def row_own(stretch_id):
        return exact_dot(row_onehot, mod_own[:, stretch_id, :])

    def input_grads(partial_rows, normed, inverse, scale):
        own_grad = column_sum(partial_rows)
        normed_own = own_cols(normed)
        scaled_grad = own_grad * (1.0 + own_cols(scale))
        mean_grad, mean_cross = lax.psum(
            (
                jnp.sum(scaled_grad, axis=1, keepdims=True) / model_width,
                jnp.sum(scaled_grad * normed_own, axis=1, keepdims=True) / model_width,
            ),
            "tp",
        )
        return (
            own_grad,
            own_grad * normed_own,
            inverse * (scaled_grad - mean_grad - normed_own * mean_cross),
        )

    picked = jnp.dot(place, jnp.concatenate([tokens, out_grad], axis=1), preferred_element_type=f32)
    rows_in = picked[:, :col_local].astype(bf16)
    grad_rows = picked[:, col_local:]
    gate_one = row_own(2)
    gate_two = row_own(5)
    mlp_grad = (grad_rows * gate_two).astype(bf16)
    full_in = whole_rows(rows_in).astype(f32)
    mlp_grad_full = whole_rows(mlp_grad)
    normed_one, inverse_one = norm_rows(full_in)
    scale_one = row_full(1)
    branch_one = (normed_one * (1.0 + scale_one) + row_full(0)).astype(bf16)
    qkv_bias = jnp.stack([qv_bias[0], jnp.zeros_like(qv_bias[0]), qv_bias[1]]).astype(f32)
    qkv_rows = (
        jnp.einsum("rd,dcf->rcf", branch_one, qkv_weight, preferred_element_type=f32)
        + qkv_bias[None]
    ).astype(bf16)
    query_all, key_all, value_all = (
        qkv_rows[:, part].reshape(ROWS, heads_local, HEAD_DIM) for part in range(3)
    )
    same_image = row_image[:, None] == row_image[None, :]
    raw = jnp.einsum("qhe,khe->hqk", query_all, key_all, preferred_element_type=f32) * scale_factor
    masked = jnp.where(same_image[None], raw, -1e30)
    top_score = jnp.max(masked, axis=2, keepdims=True)
    exp_scores = jnp.exp(masked - top_score)
    attn_probs = exp_scores / jnp.sum(exp_scores, axis=2, keepdims=True)
    probs_low = attn_probs.astype(bf16)
    attended = (
        jnp.einsum("hqk,khe->qhe", probs_low, value_all, preferred_element_type=f32)
        .reshape(ROWS, head_cols)
        .astype(bf16)
    )
    attn_out = column_sum(
        jnp.dot(attended, proj_weight, preferred_element_type=f32)
    ) + proj_bias.astype(f32)
    middle = rows_in.astype(f32) + gate_one * attn_out
    middle_full = whole_rows(middle.astype(bf16)).astype(f32)
    normed_two, inverse_two = norm_rows(middle_full)
    scale_two = row_full(4)
    branch_two = (normed_two * (1.0 + scale_two) + row_full(3)).astype(bf16)
    pre_act = jnp.dot(branch_two, hidden_weight, preferred_element_type=f32) + hidden_bias.astype(
        f32
    )
    act_low = gelu_tanh(pre_act).astype(bf16)
    mlp_out = column_sum(
        jnp.dot(act_low, output_weight, preferred_element_type=f32)
    ) + output_bias.astype(f32)
    final_rows = middle + gate_two * mlp_out
    output = reinsert(final_rows.astype(bf16), tokens)
    gate_two_rows = grad_rows * mlp_out
    output_bias_term = jnp.sum(mlp_grad, axis=0, dtype=f32)
    output_weight_term = jnp.einsum(
        "rf,rd->fd", act_low, mlp_grad_full, preferred_element_type=f32
    ).astype(bf16)
    act_grad = jnp.einsum("rd,fd->rf", mlp_grad_full, output_weight, preferred_element_type=f32)
    gelu_pull = jax.vjp(gelu_tanh, pre_act)[1]
    pre_grad = gelu_pull(act_grad)[0].astype(bf16)
    hidden_bias_term = jnp.sum(pre_grad, axis=0, dtype=f32)
    hidden_weight_term = jnp.einsum(
        "rd,rf->df", branch_two, pre_grad, preferred_element_type=f32
    ).astype(bf16)
    two_partial = jnp.einsum("rf,df->rd", pre_grad, hidden_weight, preferred_element_type=f32)
    shift_two_grad, scale_two_grad, two_norm_grad = input_grads(
        two_partial, normed_two, inverse_two, scale_two
    )
    middle_grad = grad_rows + two_norm_grad
    gate_one_rows = middle_grad * attn_out
    attn_grad = (middle_grad * gate_one).astype(bf16)
    proj_bias_term = jnp.sum(attn_grad, axis=0, dtype=f32)
    attn_grad_full = whole_rows(attn_grad)
    proj_weight_term = jnp.einsum(
        "rf,rd->fd", attended, attn_grad_full, preferred_element_type=f32
    ).astype(bf16)
    attended_grad = (
        jnp.einsum("rd,fd->rf", attn_grad_full, proj_weight, preferred_element_type=f32)
        .astype(bf16)
        .reshape(ROWS, heads_local, HEAD_DIM)
    )
    value_term = jnp.einsum("hqk,qhe->khe", probs_low, attended_grad, preferred_element_type=f32)
    prob_grad = jnp.einsum("qhe,khe->hqk", attended_grad, value_all, preferred_element_type=f32)
    row_dot = jnp.sum(attn_probs * prob_grad, axis=2, keepdims=True)
    score_grad = (attn_probs * (prob_grad - row_dot)).astype(bf16)
    query_term = (
        jnp.einsum("hqk,khe->qhe", score_grad, key_all, preferred_element_type=f32) * scale_factor
    )
    key_term = (
        jnp.einsum("hqk,qhe->khe", score_grad, query_all, preferred_element_type=f32) * scale_factor
    )
    qkv_grad = (
        jnp.stack([query_term, key_term, value_term], axis=1)
        .reshape(ROWS, 3, head_cols)
        .astype(bf16)
    )
    qkv_sums = jnp.sum(qkv_grad, axis=0, dtype=f32)
    qkv_weight_term = jnp.einsum(
        "rd,rcf->dcf", branch_one, qkv_grad, preferred_element_type=f32
    ).astype(bf16)
    one_partial = jnp.einsum("rcf,dcf->rd", qkv_grad, qkv_weight, preferred_element_type=f32)
    shift_one_grad, scale_one_grad, one_norm_grad = input_grads(
        one_partial, normed_one, inverse_one, scale_one
    )
    in_grad = middle_grad + one_norm_grad
    tokens_grad = reinsert(in_grad.astype(bf16), out_grad)
    per_row = jnp.concatenate(
        [
            shift_one_grad,
            scale_one_grad,
            gate_one_rows,
            shift_two_grad,
            scale_two_grad,
            gate_two_rows,
        ],
        axis=1,
    )
    mod_grad = jnp.einsum(
        "rw,rf->wf", row_onehot, per_row, precision=HIGHEST, preferred_element_type=f32
    )
    small = jnp.concatenate(
        [
            mod_grad.reshape(-1),
            qkv_sums[0],
            qkv_sums[2],
            proj_bias_term,
            hidden_bias_term,
            output_bias_term,
        ]
    )
    small_all = lax.all_gather(small, "seq", axis=0)
    mod_size = mod_grad.size
    mod_all = small_all[:, :mod_size].reshape(images, 6, col_local)
    bias_sums = jnp.sum(small_all[:, mod_size:], axis=0)
    ada_bias_grad = jnp.sum(mod_all, axis=0)
    qv_bias_grad = bias_sums[: 2 * col_local].reshape(2, col_local)
    at = 2 * col_local
    proj_bias_grad = bias_sums[at : at + col_local]
    at += col_local
    hidden_bias_grad = bias_sums[at : at + hidden_bias.shape[0]]
    at += hidden_bias.shape[0]
    output_bias_grad = bias_sums[at:]
    width_start = seq_index * slice_width
    cond_cols = lax.dynamic_slice_in_dim(condition, width_start, slice_width, 1)
    low_cols = lax.dynamic_slice_in_dim(cond_low, width_start, slice_width, 1)
    ada_weight_grad = jnp.einsum(
        "wd,wcf->dcf", low_cols.astype(f32), mod_all, precision=HIGHEST, preferred_element_type=f32
    )
    ada_rows = lax.dynamic_slice_in_dim(ada_weight, width_start, slice_width, 0)
    cond_grad = lax.psum(
        jnp.einsum(
            "wcf,dcf->wd",
            mod_all,
            ada_rows.astype(f32),
            precision=HIGHEST,
            preferred_element_type=f32,
        ),
        "tp",
    )
    silu_pull = jax.vjp(jax.nn.silu, cond_cols)[1]
    class_grad = jnp.einsum(
        "wc,wd->cd",
        label_hot.astype(f32),
        silu_pull(cond_grad)[0],
        precision=HIGHEST,
        preferred_element_type=f32,
    )
    qkv_weight_grad, proj_weight_grad, hidden_weight_grad, output_weight_grad = (
        lax.psum_scatter(qkv_weight_term, "seq", scatter_dimension=0, tiled=True).astype(f32),
        lax.psum_scatter(proj_weight_term, "seq", scatter_dimension=1, tiled=True).astype(f32),
        lax.psum_scatter(hidden_weight_term, "seq", scatter_dimension=0, tiled=True).astype(f32),
        lax.psum_scatter(output_weight_term, "seq", scatter_dimension=1, tiled=True).astype(f32),
    )
    return (
        output,
        tokens_grad,
        class_grad,
        ada_weight_grad,
        ada_bias_grad,
        qkv_weight_grad,
        qv_bias_grad,
        proj_weight_grad,
        proj_bias_grad,
        hidden_weight_grad,
        hidden_bias_grad,
        output_weight_grad,
        output_bias_grad,
    )


def solution(mesh):
    return jax.shard_map(
        local,
        mesh=mesh,
        in_specs=(
            P("seq", "tp"),
            P("seq", "tp"),
            P("seq"),
            P(),
            P(),
            P(),
            P(),
            P(None, None, "tp"),
            P(None, "tp"),
            P(None, None, "tp"),
            P(None, "tp"),
            P("tp", None),
            P("tp"),
            P(None, "tp"),
            P("tp"),
            P("tp", None),
            P("tp"),
        ),
        out_specs=(
            P("seq", "tp"),
            P("seq", "tp"),
            P(None, "seq"),
            P("seq", None, "tp"),
            P(None, "tp"),
            P("seq", None, "tp"),
            P(None, "tp"),
            P("tp", "seq"),
            P("tp"),
            P("seq", "tp"),
            P("tp"),
            P("tp", "seq"),
            P("tp"),
        ),
        check_vma=False,
    )
```

profile of v0, /device:TPU:0, one launch (start us, length us, event | category | flops | bytes accessed | tf_op | source)
XLA Modules:
  0.0 589.2 jit_solution(4795627765267242598)
XLA Ops:
  9.4 2.4 fusion.24
  14.4 2.9 multiply_convert_fusion.4
  17.3 3.5 convolution_add_fusion.4
  21.1 26.5 %all_gather.22 = f32[4,6,1152]{1,0,2:T(4,128)S(1)} all-gather(f32[4,6,288]{1,0,2:T(4,128)S(1)} %copy.102), channel_id=1, replica_groups=mesh['seq'=8,'tp'=4] {'tp'}, dimensions={2}, use_global_device_ids=true | all-gather | bytes 138240 | tf_op jit(solution)/shard_map/all_gather | solution.py:102
  47.6 6.0 %fusion.109 = (f32[4,1,1152]{1,0,2:T(4,128)}, f32[4,1,1152]{1,0,2:T(4,128)}, f32[4,1,1152]{1,0,2:T(4,128)}, f32[4,1,1152]{1,0,2:T(4,128)}) fusion(f32[4,6,1152]{1,0,2:T(4,128)S(1)} %all_gather.22), kind=kLoop, calls=%fused_computation.184 | loop fusion | bytes 147456 | tf_op jit(solution)/shard_map/slice | solution.py:105
  53.6 2.1 copy.105
  55.7 2.3 copy.103
  59.4 3.1 fusion.59
  66.1 3.9 fusion.21
  72.7 6.5 %fusion.113 = (f32[4,640]{1,0:T(4,128)S(1)}, f32[4,640,640]{1,2,0:T(8,128)}) fusion(pred[640,640]{0,1:T(8,128)(4,1)} %broadcast_compare_fusion, bf16[640,4,72]{0,2,1:T(8,128)(2,1)S(1)} %bitcast.99, bf16[640,4,72]{0,2,1:T(8,128)(2,1)S(1)} %bitcast.97), kind=kOutput, calls=%fused_computation.188 | convolution fusion | flops 242483840 | bytes 7710720 | tf_op jit(solution)/shard_map/sub | solution.py:150
  79.2 3.7 fusion.38
  83.7 2.2 convolution_convert_fusion.5
  85.9 2.7 convert_reduce_fusion.4
  88.8 25.1 %reduce-scatter.9.cloned.1.call-done = bf16[640,288]{0,1:T(8,128)(2,1)} async-done(((bf16[640,1152]{0,1:T(8,128)(2,1)}), bf16[640,288]{0,1:T(8,128)(2,1)}) %reduce-scatter.9.cloned.1.call-update) | async-done | bytes 368656 | tf_op jit(solution)/shard_map/reduce_scatter | solution.py:79
  113.9 2.9 fusion.78
  116.9 2.1 copy.111
  119.0 2.3 copy.109
  121.3 3.1 fusion.57
  124.4 10.8 %all-gather.10.cloned.1.call-done = bf16[640,1152]{0,1:T(8,128)(2,1)} async-done(((bf16[640,288]{0,1:T(8,128)(2,1)}), bf16[640,1152]{0,1:T(8,128)(2,1)}) %all-gather.10.cloned.1.call-update) | async-done | bytes 1474576 | tf_op jit(solution)/shard_map/all_gather | solution.py:76
  135.2 6.1 %fusion.115 = f32[640,1152]{0,1:T(8,128)} fusion(bf16[1152,1152]{1,0:T(8,128)(2,1)} %param.32, bf16[640,1152]{0,1:T(8,128)(2,1)} %all-gather.10.cloned.1.call-done), kind=kOutput, calls=%fused_computation.190 | convolution fusion | flops 1698693120 | bytes 7077888 | tf_op jit(solution)/shard_map/rd,fd->rf/dot_general | solution.py:180
  141.3 15.1 %all-gather.8.cloned.1.call-done = bf16[640,1152]{0,1:T(8,128)(2,1)} async-done(((bf16[640,288]{0,1:T(8,128)(2,1)}), bf16[640,1152]{0,1:T(8,128)(2,1)}) %all-gather.8.cloned.1.call-update) | async-done | bytes 1474576 | tf_op jit(solution)/shard_map/all_gather | solution.py:76
  160.0 3.9 fusion.11
  164.0 6.0 %convert_reduce_fusion.2 = (f32[1152]{0:T(1024)S(1)}, bf16[640,1152]{0,1:T(8,128)(2,1)S(1)}, f32[640,1152]{0,1:T(8,128)}) fusion(f32[640,1152]{0,1:T(8,128)S(1)} %copy-done.43, f32[1152]{0:T(1024)S(1)} %convert_element_type.178, bf16[640,1152]{0,1:T(8,128)(2,1)S(1)} %fusion.11, bf16[1152,1152]{1,0:T(8,128)(2,1)S(1)} %copy-done), kind=kOutput, calls=%fused_computation.42 | convolution fusion | flops 1715649408 | bytes 11510784 | tf_op jit(solution)/shard_map/dot_general | solution.py:166
  171.2 4.0 convolution_convert_fusion.3
  175.2 3.4 fusion.4
  178.6 24.3 %reduce-scatter.13.cloned.1.call-done = bf16[640,288]{0,1:T(8,128)(2,1)} async-done(((bf16[640,1152]{0,1:T(8,128)(2,1)}), bf16[640,288]{0,1:T(8,128)(2,1)}) %reduce-scatter.13.cloned.1.call-update) | async-done | bytes 368656 | tf_op jit(solution)/shard_map/reduce_scatter | solution.py:79
  204.3 5.9 all-reduce.1
  210.2 2.9 convert_reduce_fusion.5
  213.2 6.6 %convolution_convert_fusion.4 = bf16[640,1152]{0,1:T(8,128)(2,1)} fusion(bf16[1152,1152]{1,0:T(8,128)(2,1)} %param.32, f32[640,1152]{0,1:T(8,128)} %get-tuple-element.54), kind=kOutput, calls=%fused_computation.28 | convolution fusion | flops 1706065920 | bytes 7077888 | tf_op jit(solution)/shard_map/dot_general | solution.py:171
  219.8 5.4 convolution_convert_fusion.1
  225.3 5.8 convolution_convert_fusion
  231.4 2.1 all-gather.12.cloned.1.call-done
  233.5 2.4 convolution_convert_fusion.7
  237.9 4.1 multiply_reduce_fusion
  247.9 4.3 fusion.41
  252.2 3.2 fusion.9
  257.7 5.6 convolution_convert_fusion.2
  263.7 3.2 fusion.35
  267.2 71.5 %reduce-scatter.21.cloned.1.call-done = bf16[144,1152]{1,0:T(8,128)(2,1)} async-done(((bf16[1152,1152]{1,0:T(8,128)(2,1)}), bf16[144,1152]{1,0:T(8,128)(2,1)}) %reduce-scatter.21.cloned.1.call-update) | async-done | bytes 331792 | tf_op jit(solution)/shard_map/reduce_scatter | solution.py:293
  340.5 71.4 %reduce-scatter.23.cloned.1.call-done = bf16[1152,144]{0,1:T(8,128)(2,1)} async-done(((bf16[1152,1152]{0,1:T(8,128)(2,1)}), bf16[1152,144]{0,1:T(8,128)(2,1)}) %reduce-scatter.23.cloned.1.call-update) | async-done | bytes 331792 | tf_op jit(solution)/shard_map/reduce_scatter | solution.py:294
  413.8 62.3 %reduce-scatter.19.cloned.1.call-done = bf16[288,144]{0,1:T(8,128)(2,1)} async-done(((bf16[288,1152]{0,1:T(8,128)(2,1)}), bf16[288,144]{0,1:T(8,128)(2,1)}) %reduce-scatter.19.cloned.1.call-update) | async-done | bytes 82960 | tf_op jit(solution)/shard_map/reduce_scatter | solution.py:292
  477.7 27.7 %reduce-scatter.15.cloned.1.call-done = bf16[640,288]{0,1:T(8,128)(2,1)} async-done(((bf16[640,1152]{0,1:T(8,128)(2,1)}), bf16[640,288]{0,1:T(8,128)(2,1)}) %reduce-scatter.15.cloned.1.call-update) | async-done | bytes 368656 | tf_op jit(solution)/shard_map/reduce_scatter | solution.py:79
  509.6 2.3 fusion.64
  512.1 31.6 %all-gather = f32[73728]{0:T(1024)S(1)} all-gather(f32[9216]{0:T(1024)S(1)} %concatenate.21), channel_id=2, replica_groups=mesh['seq'=8,'tp'=4] {'seq'}, dimensions={0}, use_global_device_ids=true | all-gather | bytes 331776 | tf_op jit(solution)/shard_map/all_gather | solution.py:253
  548.1 11.1 %all-reduce = (f32[640]{0:T(1024)S(1)}, f32[640]{0:T(1024)S(1)}, f32[32,144]{1,0:T(8,128)S(1)}) all-reduce(f32[640]{0:T(1024)S(1)} %broadcast_multiply_fusion, f32[640]{0:T(1024)S(1)} %broadcast_multiply_fusion.1, f32[32,144]{1,0:T(8,128)S(1)} %convolution_bitcast_fusion.1), channel_id=1, replica_groups=mesh['seq'=8,'tp'=4] {'tp'}, use_global_device_ids=true, to_apply=%region_22.23 | all-reduce | flops 5888 | bytes 47104 | tf_op jit(solution)/shard_map/psum | solution.py:114
  559.9 2.1 fusion.73
  563.9 3.5 fusion.34
  567.3 12.9 %reduce-scatter.17.cloned.1.call-done = bf16[144,3,288]{2,0,1:T(8,128)(2,1)} async-done(((bf16[1152,3,288]{2,0,1:T(8,128)(2,1)}), bf16[144,3,288]{2,0,1:T(8,128)(2,1)}) %reduce-scatter.17.cloned.1.call-update) | async-done | bytes 248848 | tf_op jit(solution)/shard_map/reduce_scatter | solution.py:291
  (186 shorter events, 49.3 us)
Async XLA Ops:
  7.2 156.8 %copy-start = (bf16[1152,1152]{1,0:T(8,128)(2,1)S(1)}, bf16[1152,1152]{1,0:T(8,128)(2,1)}, u32[]{:S(2)}) copy-start(bf16[1152,1152]{1,0:T(8,128)(2,1)} %param.30) | copy-start | bytes 7962628
  7.2 55.3 %all-gather.6.cloned.1.call-start = ((), (), s32[]{:S(2)}) async-start(), calls=%async_computation.8 | async-start | bytes 1843200 | tf_op jit(solution)/shard_map/all_gather | solution.py:76
  9.3 4.4 copy-start.37
  9.3 4.7 copy-start.38
  9.3 4.7 copy-start.27
  9.3 5.1 copy-start.29
  13.7 100.2 %reduce-scatter.9.cloned.1.call-start = ((), (), s32[]{:S(2)}) async-start(), calls=%async_computation.9 | async-start | bytes 1843200 | tf_op jit(solution)/shard_map/reduce_scatter | solution.py:79
  53.6 4.6 copy-start.26
  62.5 3.6 copy-start.2
  66.1 3.9 copy-start.32
  72.7 6.5 %copy-start.16 = (bf16[640,1,288]{0,2,1:T(8,128)(2,1)}, bf16[640,1,288]{0,2,1:T(8,128)(2,1)S(1)}, u32[]{:S(2)}) copy-start(bf16[640,1,288]{0,2,1:T(8,128)(2,1)S(1)} %get-tuple-element.38) | copy-start | bytes 1105924
  72.7 6.5 %copy-start.17 = (bf16[640,1,288]{0,2,1:T(8,128)(2,1)}, bf16[640,1,288]{0,2,1:T(8,128)(2,1)S(1)}, u32[]{:S(2)}) copy-start(bf16[640,1,288]{0,2,1:T(8,128)(2,1)S(1)} %get-tuple-element.39) | copy-start | bytes 1105924
  79.2 4.5 copy-start.36
  83.7 5.1 copy-start.30
  85.9 31.0 %copy-start.28 = (bf16[1152]{0:T(1024)(128)(2,1)S(1)}, bf16[1152]{0:T(1024)(128)(2,1)}, u32[]{:S(2)}) copy-start(bf16[1152]{0:T(1024)(128)(2,1)} %param.31) | copy-start | bytes 6916
  85.9 49.3 %all-gather.10.cloned.1.call-start = ((), (), s32[]{:S(2)}) async-start(), calls=%async_computation.12 | async-start | bytes 1843200 | tf_op jit(solution)/shard_map/all_gather | solution.py:76
  88.7 67.7 %all-gather.8.cloned.1.call-start = ((), (), s32[]{:S(2)}) async-start(), calls=%async_computation.10 | async-start | bytes 1843200 | tf_op jit(solution)/shard_map/all_gather | solution.py:76
  116.8 86.1 %reduce-scatter.13.cloned.1.call-start = ((), (), s32[]{:S(2)}) async-start(), calls=%async_computation.13 | async-start | bytes 1843200 | tf_op jit(solution)/shard_map/reduce_scatter | solution.py:79
  156.4 3.6 copy-start.4
  160.0 4.0 copy-start.43
  164.0 6.0 %copy-start.12 = (bf16[640,1152]{0,1:T(8,128)(2,1)}, bf16[640,1152]{0,1:T(8,128)(2,1)S(1)}, u32[]{:S(2)}) copy-start(bf16[640,1152]{0,1:T(8,128)(2,1)S(1)} %fusion.11) | copy-start | bytes 4423684
  175.2 27.7 %copy-start.5 = (f32[640,1152]{0,1:T(8,128)S(1)}, f32[640,1152]{0,1:T(8,128)}, u32[]{:S(2)}) copy-start(f32[640,1152]{0,1:T(8,128)} %fusion.57) | copy-start | bytes 8847364
  175.2 58.3 %all-gather.12.cloned.1.call-start = ((), (), s32[]{:S(2)}) async-start(), calls=%async_computation.14 | async-start | bytes 1843200 | tf_op jit(solution)/shard_map/all_gather | solution.py:76
  213.1 50.6 %reduce-scatter.11.cloned.1.call-start = ((), (), s32[]{:S(2)}) async-start(), calls=%async_computation.11 | async-start | bytes 1843200 | tf_op jit(solution)/shard_map/reduce_scatter | solution.py:79
  213.2 6.7 %copy-start.13 = (bf16[640,1152]{0,1:T(8,128)(2,1)S(1)}, bf16[640,1152]{0,1:T(8,128)(2,1)}, u32[]{:S(2)}) copy-start(bf16[640,1152]{0,1:T(8,128)(2,1)} %copy-done.12) | copy-start | bytes 4423684
  219.8 5.6 copy-start.34
  219.8 118.9 %reduce-scatter.21.cloned.1.call-start = ((), (), s32[]{:S(2)}) async-start(), calls=%async_computation.18 | async-start | bytes 2985984 | tf_op jit(solution)/shard_map/reduce_scatter | solution.py:293
  225.3 186.7 %reduce-scatter.23.cloned.1.call-start = ((), (), s32[]{:S(2)}) async-start(), calls=%async_computation.19 | async-start | bytes 2985984 | tf_op jit(solution)/shard_map/reduce_scatter | solution.py:294
  231.2 4.7 copy-start.40
  231.2 244.9 %reduce-scatter.19.cloned.1.call-start = ((), (), s32[]{:S(2)}) async-start(), calls=%async_computation.17 | async-start | bytes 995328 | tf_op jit(solution)/shard_map/reduce_scatter | solution.py:292
  235.9 6.1 %copy-start.41 = (bf16[640,288]{0,1:T(8,128)(2,1)}, bf16[640,288]{0,1:T(8,128)(2,1)S(1)}, u32[]{:S(2)}) copy-start(bf16[640,288]{0,1:T(8,128)(2,1)S(1)} %convolution_convert_fusion.7) | copy-start | bytes 1105924
  237.9 4.3 slice-start
  237.9 5.1 slice-start.1
  246.0 259.4 %reduce-scatter.15.cloned.1.call-start = ((), (), s32[]{:S(2)}) async-start(), calls=%async_computation.15 | async-start | bytes 1843200 | tf_op jit(solution)/shard_map/reduce_scatter | solution.py:79
  247.8 4.4 copy-start.20
  247.8 4.4 copy-start.19
  247.8 4.4 copy-start.33
  252.2 3.3 copy-start.24
  252.2 3.5 copy-start.31
  252.2 3.5 copy-start.3
  255.5 324.8 %reduce-scatter.17.cloned.1.call-start = ((), (), s32[]{:S(2)}) async-start(), calls=%async_computation.16 | async-start | bytes 2985984 | tf_op jit(solution)/shard_map/reduce_scatter | solution.py:291
  257.7 6.0 %copy-start.7 = (f32[640,576]{0,1:T(8,128)S(1)}, f32[640,576]{0,1:T(8,128)}, u32[]{:S(2)}) copy-start(f32[640,576]{0,1:T(8,128)} %copy-done.6) | copy-start | bytes 4423684
  257.7 6.0 %copy-start.10 = (f32[640,288]{0,1:T(8,128)S(1)}, f32[640,288]{0,1:T(8,128)}, u32[]{:S(2)}) copy-start(f32[640,288]{0,1:T(8,128)} %get-tuple-element.52) | copy-start | bytes 2211844
  257.7 6.0 %copy-start.14 = (bf16[640,288]{0,1:T(8,128)(2,1)S(1)}, bf16[640,288]{0,1:T(8,128)(2,1)}, u32[]{:S(2)}) copy-start(bf16[640,288]{0,1:T(8,128)(2,1)} %reduce-scatter.9.cloned.1.call-done) | copy-start | bytes 1105924
  267.2 240.9 %copy-start.9 = (f32[640,288]{0,1:T(8,128)S(1)}, f32[640,288]{0,1:T(8,128)}, u32[]{:S(2)}) copy-start(f32[640,288]{0,1:T(8,128)} %get-tuple-element.30) | copy-start | bytes 2211844
  413.8 94.4 %copy-start.8 = (bf16[640,288]{0,1:T(8,128)(2,1)S(1)}, bf16[640,288]{0,1:T(8,128)(2,1)}, u32[]{:S(2)}) copy-start(bf16[640,288]{0,1:T(8,128)(2,1)} %reduce-scatter.13.cloned.1.call-done) | copy-start | bytes 1105924
  543.7 20.1 %copy-start.15 = (bf16[640,288]{0,1:T(8,128)(2,1)S(1)}, bf16[640,288]{0,1:T(8,128)(2,1)}, u32[]{:S(2)}) copy-start(bf16[640,288]{0,1:T(8,128)(2,1)} %reduce-scatter.15.cloned.1.call-done) | copy-start | bytes 1105924
  562.0 20.1 %copy-start.1 = (bf16[1152,1152]{1,0:T(8,128)(2,1)S(1)}, bf16[1152,1152]{1,0:T(8,128)(2,1)}, u32[]{:S(2)}) copy-start(bf16[1152,1152]{1,0:T(8,128)(2,1)} %param.30) | copy-start | bytes 7962628
  (11 other events, 18.8 us)
Sparse Core Ops, SparseCore 0:
  13.8 29.6 all-gather.5
  86.0 27.8 reduce-scatter.8
  116.1 19.0 all-gather.9
  137.3 19.0 all-gather.7
  175.3 27.5 reduce-scatter.12
  213.2 20.2 all-gather.11
  236.1 27.5 reduce-scatter.10
  267.8 70.8 reduce-scatter.20
  342.4 69.5 reduce-scatter.22
  416.2 59.8 reduce-scatter.18
  478.9 26.4 reduce-scatter.14
  508.9 71.3 reduce-scatter.16
where the time goes:
time: 595 us; the launch traced here: 589 us
  waiting for transfers between devices  324 us (54%)
  matrix products  117 us (20%)
  blocking collectives  75 us (13%)
  other arithmetic  33.7 us (6%)
  local copies, waits for them, and re-layouts  23.8 us (4%)
  between operations  15.1 us (3%)
    reduce_scatter x4, waiting for transfers between devices, column_sum(): lax.psum_scatter(part_rows.astype(bf16), 'tp', scatter_dimension=1, tiled...  77.5 us
    reduce_scatter x1, waiting for transfers between devices, local(): lax.psum_scatter(hidden_weight_term, 'seq', scatter_dimension=0, tiled=True)  71.5 us
    reduce_scatter x1, waiting for transfers between devices, local(): lax.psum_scatter(output_weight_term, 'seq', scatter_dimension=1, tiled=True)  71.4 us
    reduce_scatter x1, waiting for transfers between devices, local(): lax.psum_scatter(proj_weight_term, 'seq', scatter_dimension=1, tiled=True)  62.3 us
    all_gather x1, blocking collectives, local(): small_all = lax.all_gather(small, 'seq', axis=0)  31.6 us
    all_gather x4, waiting for transfers between devices, whole_rows(): return lax.all_gather(part_rows, 'tp', axis=1, tiled=True)  28 us
    all_gather x1, blocking collectives, local(): mod_full = lax.all_gather(mod_own, 'tp', axis=2, tiled=True)  26.5 us
    dot_general x6, matrix products, exact_dot(): jnp.dot(left_mat, right_mat, precision=HIGHEST, preferred_element_type=jn...  19.7 us
  transfers between devices with their start and end apart: 12, of which 11 were waited for; matrix products, arithmetic and copies ran while one was open for 20% of the time, Pallas kernels for 0%

commit v1 on v0

--- a/solution.py
+++ b/solution.py
@@ -9,6 +9,15 @@
 ROWS = 640
 NORM_EPS = 1e-06
 HIGHEST = lax.Precision.HIGHEST
+
+
+def launch_pools(vals, in_dim):
+    vals = jnp.moveaxis(vals, 0, in_dim)
+    wide_out = vals.shape
+    carry_out = vals.reshape(
+        *wide_out[:in_dim], wide_out[in_dim] * wide_out[in_dim + 1], *wide_out[in_dim + 2 :]
+    )
+    return carry_out
 
 
 def exact_dot(left_mat, right_mat):
@@ -73,7 +82,32 @@
     row_onehot = (row_image[:, None] == jnp.arange(IMG_DEV, dtype=jnp.int32)[None, :]).astype(f32)
 
     def whole_rows(part_rows):
-        return lax.all_gather(part_rows, "tp", axis=1, tiled=True)
+
+        def _raise_shards(slab_in, net_axis, out_dim):
+            n_blocks = lax.axis_size(net_axis)
+            table = list(map(lambda ii: (ii, (ii + 1) % n_blocks), range(n_blocks)))
+            bank = [(k0, m) for m, k0 in table]
+            piece_now, v_next = ([], [])
+            for u in [*range(n_blocks - 1)]:
+                if u % 2 == 0:
+                    piece_now.append(
+                        lax.ppermute(
+                            piece_now[-1] if piece_now else slab_in, axis_name=net_axis, perm=table
+                        )
+                    )
+                else:
+                    q_next = lax.ppermute(
+                        v_next[-1] if v_next else slab_in, axis_name=net_axis, perm=bank
+                    )
+                    v_next.append(q_next)
+            part_now = jnp.stack([*piece_now[::-1], slab_in, *v_next])
+            shaped = lax.axis_index(net_axis)
+            val = shaped - len(piece_now)
+            part_now = part_now[(jnp.arange(n_blocks) - val) % n_blocks]
+            item_now = launch_pools(part_now, out_dim)
+            return item_now
+
+        return _raise_shards(part_rows, net_axis="tp", out_dim=1)
 
     def column_sum(part_rows):
         return lax.psum_scatter(

time: 595 us -> 567 us (0.953)
  waiting for transfers between devices: 324 us -> 277 us
  local copies, waits for them, and re-layouts: 23.8 us -> 41.5 us
  matrix products: 117 us -> 107 us
  starting transfers between devices: 0.88 us -> 10 us
  other arithmetic: 33.7 us -> 42.6 us
  blocking collectives: 75 us -> 67.1 us
    reduce_scatter x1, waiting for transfers between devices: 62.3 us -> 19.7 us  [local(): lax.psum_scatter(proj_weight_term, 'seq', scatter_dimension=1, tiled=True)]
    all_gather x4 -> x0, waiting for transfers between devices: 28 us -> none  [whole_rows(): return lax.all_gather(part_rows, 'tp', axis=1, tiled=True)]
    ppermute x0 -> x12, waiting for transfers between devices: none -> 27.8 us  [the longest x8 27.2 us: _raise_shards(): lax.ppermute(piece_now[-1] if piece_now else slab_in, axis_name=net_axis,...]
    gather x0 -> x4, local copies, waits for them, and re-layouts: none -> 13.1 us  [_raise_shards(): part_now = part_now[(jnp.arange(n_blocks) - val) % n_blocks]]
    ppermute x0 -> x12, starting transfers between devices: none -> 9.29 us  [the longest x4 7.14 us: _raise_shards(): lax.ppermute(v_next[-1] if v_next else slab_in, axis_name=net_axis, perm=...]
    another operation x3 -> x7, other arithmetic: 1.32 us -> 10.6 us  [the longest x4 9.24 us: _raise_shards(): part_now = jnp.stack([*piece_now[::-1], slab_in, *v_next])]
    all_gather x1, blocking collectives: 26.5 us -> 18 us  [local(): mod_full = lax.all_gather(mod_own, 'tp', axis=2, tiled=True)]
  transfers between devices with their start and end apart: 12 -> 20, of which waited for: 11 -> 13; matrix products, arithmetic and copies ran while one was open for 20% -> 23% of each run, Pallas kernels for 0% -> 0%
where the time goes in v1:
time: 567 us; the launch traced here: 561 us
  waiting for transfers between devices  277 us (49%)
  matrix products  107 us (19%)
  blocking collectives  67.1 us (12%)
  other arithmetic  42.6 us (8%)
  local copies, waits for them, and re-layouts  41.5 us (7%)
  between operations  15.2 us (3%)
  starting transfers between devices  10 us (2%)
    reduce_scatter x4, waiting for transfers between devices, column_sum(): lax.psum_scatter(part_rows.astype(bf16), 'tp', scatter_dimension=1, tiled...  73.9 us
    reduce_scatter x1, waiting for transfers between devices, local(): lax.psum_scatter(output_weight_term, 'seq', scatter_dimension=1, tiled=True)  71.7 us
    reduce_scatter x1, waiting for transfers between devices, local(): lax.psum_scatter(hidden_weight_term, 'seq', scatter_dimension=0, tiled=True)  71.3 us
    all_gather x1, blocking collectives, local(): small_all = lax.all_gather(small, 'seq', axis=0)  31.7 us
    ppermute x8, waiting for transfers between devices, _raise_shards(): lax.ppermute(piece_now[-1] if piece_now else slab_in, axis_name=net_axis,...  27.2 us
    reduce_scatter x1, waiting for transfers between devices, local(): lax.psum_scatter(proj_weight_term, 'seq', scatter_dimension=1, tiled=True)  19.7 us
    all_gather x1, blocking collectives, local(): mod_full = lax.all_gather(mod_own, 'tp', axis=2, tiled=True)  18 us
    psum x2, blocking collectives, input_grads(): lax.psum((jnp.sum(scaled_grad, axis=1, keepdims=True) / model_width, jnp....  17.4 us
  transfers between devices with their start and end apart: 20, of which 13 were waited for; matrix products, arithmetic and copies ran while one was open for 23% of the time, Pallas kernels for 0%

profile of v1, /device:TPU:0, one launch (start us, length us, event | category | flops | bytes accessed | tf_op | source)
XLA Modules:
  0.0 560.6 jit_solution(2905351657933143893)
XLA Ops:
  9.9 2.4 fusion.20
  20.7 3.5 convolution_add_fusion.4
  24.5 18.0 %all_gather.9 = f32[4,6,1152]{1,0,2:T(4,128)S(1)} all-gather(f32[4,6,288]{1,0,2:T(4,128)S(1)} %copy.102), channel_id=1, replica_groups=mesh['seq'=8,'tp'=4] {'tp'}, dimensions={2}, use_global_device_ids=true | all-gather | bytes 138240 | tf_op jit(solution)/shard_map/all_gather | solution.py:136
  42.5 6.0 %fusion.107 = (f32[4,1,1152]{1,0,2:T(4,128)}, f32[4,1,1152]{1,0,2:T(4,128)}, f32[4,1,1152]{1,0,2:T(4,128)}, f32[4,1,1152]{1,0,2:T(4,128)}) fusion(f32[4,6,1152]{1,0,2:T(4,128)S(1)} %all_gather.9), kind=kLoop, calls=%fused_computation.197 | loop fusion | bytes 147456 | tf_op jit(solution)/shard_map/slice | solution.py:139
  54.7 3.0 fusion.55
  57.7 3.7 collective-permute-done.1
  61.5 2.5 pad_maximum_fusion
  63.9 3.2 gather_fusion
  76.6 7.0 %fusion.111 = (f32[4,640]{1,0:T(4,128)}, f32[4,640,640]{1,2,0:T(8,128)}) fusion(pred[640,640]{0,1:T(8,128)(4,1)} %broadcast_compare_fusion, bf16[640,4,72]{0,2,1:T(8,128)(2,1)S(1)} %bitcast.141, bf16[640,4,72]{0,2,1:T(8,128)(2,1)S(1)} %bitcast.139), kind=kOutput, calls=%fused_computation.201 | convolution fusion | flops 242483840 | bytes 7710720 | tf_op jit(solution)/shard_map/sub | solution.py:184
  83.6 3.6 fusion.34
  90.3 3.3 convert_reduce_fusion.4
  93.6 24.6 %reduce-scatter.9.cloned.1.call-done = bf16[640,288]{0,1:T(8,128)(2,1)} async-done(((bf16[640,1152]{0,1:T(8,128)(2,1)}), bf16[640,288]{0,1:T(8,128)(2,1)}) %reduce-scatter.9.cloned.1.call-update) | async-done | bytes 368656 | tf_op jit(solution)/shard_map/reduce_scatter | solution.py:113
  118.2 2.7 fusion.74
  123.9 2.7 copy.111
  126.7 2.7 copy.109
  131.7 3.8 fusion.53
  135.6 3.2 collective-permute-done.7
  138.8 2.7 pad_maximum_fusion.2
  141.4 3.3 gather_fusion.2
  144.7 2.7 pad_maximum_fusion.1
  147.4 3.2 gather_fusion.1
  158.2 2.6 convolution_add_fusion.2
  160.9 4.2 convert_reduce_fusion
  166.2 3.9 convolution_convert_fusion.3
  170.2 5.6 %convolution_convert_fusion.4 = bf16[640,1152]{0,1:T(8,128)(2,1)} fusion(bf16[1152,1152]{1,0:T(8,128)(2,1)S(1)} %copy-done, f32[640,1152]{0,1:T(8,128)} %copy-done.56), kind=kOutput, calls=%fused_computation.24 | convolution fusion | flops 1706065920 | bytes 7077888 | tf_op jit(solution)/shard_map/dot_general | solution.py:205
  175.9 21.7 %reduce-scatter.13.cloned.1.call-done = bf16[640,288]{0,1:T(8,128)(2,1)} async-done(((bf16[640,1152]{0,1:T(8,128)(2,1)}), bf16[640,288]{0,1:T(8,128)(2,1)}) %reduce-scatter.13.cloned.1.call-update) | async-done | bytes 368656 | tf_op jit(solution)/shard_map/reduce_scatter | solution.py:113
  199.3 5.9 %all-reduce.1 = (f32[640]{0:T(1024)S(1)}, f32[640]{0:T(1024)S(1)}) all-reduce(f32[640]{0:T(1024)S(1)} %get-tuple-element.56, f32[640]{0:T(1024)S(1)} %get-tuple-element.57), channel_id=1, replica_groups=mesh['seq'=8,'tp'=4] {'tp'}, use_global_device_ids=true, to_apply=%region_16.17 | all-reduce | flops 1280 | bytes 10240 | tf_op jit(solution)/shard_map/psum | solution.py:148
  208.8 7.1 %collective-permute-done.9 = bf16[640,288]{0,1:T(8,128)(2,1)S(1)} collective-permute-done((bf16[640,288]{0,1:T(8,128)(2,1)S(1)}, bf16[640,288]{0,1:T(8,128)(2,1)S(1)}, u32[]{:S(2)}, u32[]{:S(2)}) %collective-permute-start.9) | collective-permute-done | bytes 368672 | tf_op jit(solution)/shard_map/ppermute | solution.py:94
  217.3 12.8 %collective-permute-done.10 = bf16[640,288]{0,1:T(8,128)(2,1)S(1)} collective-permute-done((bf16[640,288]{0,1:T(8,128)(2,1)S(1)}, bf16[640,288]{0,1:T(8,128)(2,1)S(1)}, u32[]{:S(2)}, u32[]{:S(2)}) %collective-permute-start.10) | collective-permute-done | bytes 368672 | tf_op jit(solution)/shard_map/ppermute | solution.py:94
  231.5 3.4 gather_fusion.3
  234.9 3.3 convolution_convert_fusion.6
  238.3 6.2 %convolution_convert_fusion = bf16[1152,1152]{0,1:T(8,128)(2,1)} fusion(bf16[640,1152]{0,1:T(8,128)(2,1)} %bitcast.134, f32[640,1152]{0,1:T(8,128)} %copy-done.56), kind=kOutput, calls=%fused_computation.5 | convolution fusion | flops 1706655744 | bytes 7077888 | tf_op jit(solution)/shard_map/rf,rd->fd/dot_general | solution.py:211
  244.6 5.8 %convolution_convert_fusion.1 = bf16[1152,1152]{1,0:T(8,128)(2,1)} fusion(bf16[640,1152]{0,1:T(8,128)(2,1)} %copy-done.17, bf16[640,1152]{0,1:T(8,128)(2,1)} %copy-done.57), kind=kOutput, calls=%fused_computation.6 | convolution fusion | flops 1700020224 | bytes 5603328 | tf_op jit(solution)/shard_map/rd,rf->df/dot_general | solution.py:218
  250.6 2.3 convolution_convert_fusion.7
  253.0 6.9 %multiply_reduce_fusion = (f32[4,640]{1,0:T(4,128)S(1)}, f32[4,640,640]{1,2,0:T(8,128)}) fusion(f32[4,640,640]{1,2,0:T(8,128)} %get-tuple-element.50, f32[4,640]{1,0:T(4,128)S(1)} %copy-done.33, bf16[640,4,72]{0,2,1:T(8,128)(2,1)S(1)} %bitcast.162, bf16[640,4,72]{0,2,1:T(8,128)(2,1)S(1)} %bitcast.150), kind=kOutput, calls=%fused_computation.8 | convolution fusion | flops 240842240 | bytes 13864960 | tf_op jit(solution)/shard_map/qhe,khe->hqk/dot_general | solution.py:239
  259.9 4.0 multiply_convert_fusion
  267.6 3.1 fusion.5
  271.1 5.4 convolution_convert_fusion.2
  277.5 3.1 fusion.31
  280.9 19.7 %reduce-scatter.19.cloned.1.call-done = bf16[288,144]{0,1:T(8,128)(2,1)} async-done(((bf16[288,1152]{0,1:T(8,128)(2,1)}), bf16[288,144]{0,1:T(8,128)(2,1)}) %reduce-scatter.19.cloned.1.call-update) | async-done | bytes 82960 | tf_op jit(solution)/shard_map/reduce_scatter | solution.py:326
  302.3 71.7 %reduce-scatter.23.cloned.1.call-done = bf16[1152,144]{0,1:T(8,128)(2,1)} async-done(((bf16[1152,1152]{0,1:T(8,128)(2,1)}), bf16[1152,144]{0,1:T(8,128)(2,1)}) %reduce-scatter.23.cloned.1.call-update) | async-done | bytes 331792 | tf_op jit(solution)/shard_map/reduce_scatter | solution.py:328
  375.8 71.3 %reduce-scatter.21.cloned.1.call-done = bf16[144,1152]{1,0:T(8,128)(2,1)} async-done(((bf16[1152,1152]{1,0:T(8,128)(2,1)}), bf16[144,1152]{1,0:T(8,128)(2,1)}) %reduce-scatter.21.cloned.1.call-update) | async-done | bytes 331792 | tf_op jit(solution)/shard_map/reduce_scatter | solution.py:327
  449.0 27.5 %reduce-scatter.15.cloned.1.call-done = bf16[640,288]{0,1:T(8,128)(2,1)} async-done(((bf16[640,1152]{0,1:T(8,128)(2,1)}), bf16[640,288]{0,1:T(8,128)(2,1)}) %reduce-scatter.15.cloned.1.call-update) | async-done | bytes 368656 | tf_op jit(solution)/shard_map/reduce_scatter | solution.py:113
  483.4 31.7 %all-gather = f32[73728]{0:T(1024)S(1)} all-gather(f32[9216]{0:T(1024)S(1)} %concatenate.21), channel_id=2, replica_groups=mesh['seq'=8,'tp'=4] {'seq'}, dimensions={0}, use_global_device_ids=true | all-gather | bytes 331776 | tf_op jit(solution)/shard_map/all_gather | solution.py:287
  519.5 11.5 %all-reduce = (f32[640]{0:T(1024)S(1)}, f32[640]{0:T(1024)}, f32[32,144]{1,0:T(8,128)S(1)}) all-reduce(f32[640]{0:T(1024)S(1)} %broadcast_multiply_fusion, f32[640]{0:T(1024)S(1)} %broadcast_multiply_fusion.1, f32[32,144]{1,0:T(8,128)S(1)} %convolution_bitcast_fusion.1), channel_id=1, replica_groups=mesh['seq'=8,'tp'=4] {'tp'}, use_global_device_ids=true, to_apply=%region_22.23 | all-reduce | flops 5888 | bytes 47104 | tf_op jit(solution)/shard_map/psum | solution.py:148
  533.0 2.6 fusion.57
  535.6 3.5 fusion.30
  539.1 12.6 %reduce-scatter.17.cloned.1.call-done = bf16[144,3,288]{2,0,1:T(8,128)(2,1)} async-done(((bf16[1152,3,288]{2,0,1:T(8,128)(2,1)}), bf16[144,3,288]{2,0,1:T(8,128)(2,1)}) %reduce-scatter.17.cloned.1.call-update) | async-done | bytes 248848 | tf_op jit(solution)/shard_map/reduce_scatter | solution.py:325
  (235 shorter events, 77.9 us)
Async XLA Ops:
  7.2 153.7 %copy-start = (bf16[1152,1152]{1,0:T(8,128)(2,1)S(1)}, bf16[1152,1152]{1,0:T(8,128)(2,1)}, u32[]{:S(2)}) copy-start(bf16[1152,1152]{1,0:T(8,128)(2,1)} %param.32) | copy-start | bytes 7962628
  7.2 111.0 %reduce-scatter.9.cloned.1.call-start = ((), (), s32[]{:S(2)}) async-start(), calls=%async_computation.8 | async-start | bytes 1843200 | tf_op jit(solution)/shard_map/reduce_scatter | solution.py:113
  9.9 6.8 %copy-start.52 = (s32[32]{0:T(128)S(1)}, s32[32]{0:T(128)}, u32[]{:S(2)}) copy-start(s32[32]{0:T(128)} %param.20) | copy-start | bytes 388
  9.9 7.1 %copy-start.53 = (s32[32]{0:T(128)S(1)}, s32[32]{0:T(128)}, u32[]{:S(2)}) copy-start(s32[32]{0:T(128)} %param.22) | copy-start | bytes 388
  9.9 7.1 %copy-start.38 = (bf16[2,288]{1,0:T(2,128)(2,1)S(1)}, bf16[2,288]{1,0:T(2,128)(2,1)}, u32[]{:S(2)}) copy-start(bf16[2,288]{1,0:T(2,128)(2,1)} %param.27) | copy-start | bytes 3460
  9.9 7.2 %copy-start.39 = (bf16[6,288]{1,0:T(8,128)(2,1)S(1)}, bf16[6,288]{1,0:T(8,128)(2,1)}, u32[]{:S(2)}) copy-start(bf16[6,288]{1,0:T(8,128)(2,1)} %param.25) | copy-start | bytes 10372
  9.9 8.6 %copy-start.43 = (s32[32]{0:T(128)S(1)}, s32[32]{0:T(128)}, u32[]{:S(2)}) copy-start(s32[32]{0:T(128)} %param.21) | copy-start | bytes 388
  14.3 39.8 %collective-permute-start = (bf16[640,288]{0,1:T(8,128)(2,1)}, bf16[640,288]{0,1:T(8,128)(2,1)}, u32[]{:S(2)}, u32[]{:S(2)}) collective-permute-start(bf16[640,288]{0,1:T(8,128)(2,1)} %slice.142), channel_id=1, source_target_pairs={{0,1},{1,2},{2,3},{3,0},{4,5},{5,6},{6,7},{7,4},{8,9},{9,10},{10,1... | collective-permute-start | bytes 1105928 | tf_op jit(solution)/shard_map/ppermute | solution.py:94
  14.7 43.0 %collective-permute-start.2 = (bf16[640,288]{0,1:T(8,128)(2,1)}, bf16[640,288]{0,1:T(8,128)(2,1)}, u32[]{:S(2)}, u32[]{:S(2)}) collective-permute-start(bf16[640,288]{0,1:T(8,128)(2,1)} %slice.142), channel_id=1, source_target_pairs={{1,0},{2,1},{3,2},{0,3},{5,4},{6,5},{7,6},{4,7},{9,8},{10,9},{11,1... | collective-permute-start | bytes 1105928 | tf_op jit(solution)/shard_map/ppermute | solution.py:99
  20.7 21.8 %copy-start.31 = (bf16[32,1152]{1,0:T(8,128)(2,1)}, bf16[32,1152]{1,0:T(8,128)(2,1)S(1)}, u32[]{:S(2)}) copy-start(bf16[32,1152]{1,0:T(8,128)(2,1)S(1)} %get-tuple-element.47) | copy-start | bytes 221188
  24.2 24.3 %copy-start.30 = (f32[4,6,288]{2,0,1:T(4,128)}, f32[4,6,288]{2,0,1:T(4,128)S(1)}, u32[]{:S(2)}) copy-start(f32[4,6,288]{2,0,1:T(4,128)S(1)} %convolution_add_fusion.4) | copy-start | bytes 82948
  54.1 7.4 %collective-permute-start.1 = (bf16[640,288]{0,1:T(8,128)(2,1)}, bf16[640,288]{0,1:T(8,128)(2,1)S(1)}, u32[]{:S(2)}, u32[]{:S(2)}) collective-permute-start(bf16[640,288]{0,1:T(8,128)(2,1)} %collective-permute-done), channel_id=1, source_target_pairs={{0,1},{1,2},{2,3},{3,0},{4,5},{5,6},{6,7},{7,4},{8,9},{9,10},{10,1... | collective-permute-start | bytes 1105928 | tf_op jit(solution)/shard_map/ppermute | solution.py:94
  54.7 92.7 %copy-start.34 = (s32[1024]{0:T(1024)}, s32[1024]{0:T(1024)S(1)}, u32[]{:S(2)}) copy-start(s32[1024]{0:T(1024)S(1)} %pad_clamp_fusion) | copy-start | bytes 12292
  76.6 7.0 %copy-start.18 = (bf16[640,1,288]{0,2,1:T(8,128)(2,1)}, bf16[640,1,288]{0,2,1:T(8,128)(2,1)S(1)}, u32[]{:S(2)}) copy-start(bf16[640,1,288]{0,2,1:T(8,128)(2,1)S(1)} %get-tuple-element.38) | copy-start | bytes 1105924
  76.6 7.0 %copy-start.20 = (bf16[640,1,288]{0,2,1:T(8,128)(2,1)}, bf16[640,1,288]{0,2,1:T(8,128)(2,1)S(1)}, u32[]{:S(2)}) copy-start(bf16[640,1,288]{0,2,1:T(8,128)(2,1)S(1)} %get-tuple-element.39) | copy-start | bytes 1105924
  83.6 4.4 copy-start.51
  88.0 5.6 copy-start.45
  90.2 107.4 %reduce-scatter.13.cloned.1.call-start = ((), (), s32[]{:S(2)}) async-start(), calls=%async_computation.10 | async-start | bytes 1843200 | tf_op jit(solution)/shard_map/reduce_scatter | solution.py:113
  93.6 29.1 %collective-permute-start.6 = (bf16[640,288]{0,1:T(8,128)(2,1)}, bf16[640,288]{0,1:T(8,128)(2,1)}, u32[]{:S(2)}, u32[]{:S(2)}) collective-permute-start(bf16[640,288]{0,1:T(8,128)(2,1)} %get-tuple-element.25), channel_id=1, source_target_pairs={{0,1},{1,2},{2,3},{3,0},{4,5},{5,6},{6,7},{7,4},{8,9},{9,10},{10,1... | collective-permute-start | bytes 1105928 | tf_op jit(solution)/shard_map/ppermute | solution.py:94
  120.9 10.6 %collective-permute-start.3 = (bf16[640,288]{0,1:T(8,128)(2,1)}, bf16[640,288]{0,1:T(8,128)(2,1)}, u32[]{:S(2)}, u32[]{:S(2)}) collective-permute-start(bf16[640,288]{0,1:T(8,128)(2,1)} %get-tuple-element.51), channel_id=1, source_target_pairs={{0,1},{1,2},{2,3},{3,0},{4,5},{5,6},{6,7},{7,4},{8,9},{9,10},{10,1... | collective-permute-start | bytes 1105928 | tf_op jit(solution)/shard_map/ppermute | solution.py:94
  120.9 14.7 %collective-permute-start.8 = (bf16[640,288]{0,1:T(8,128)(2,1)}, bf16[640,288]{0,1:T(8,128)(2,1)}, u32[]{:S(2)}, u32[]{:S(2)}) collective-permute-start(bf16[640,288]{0,1:T(8,128)(2,1)} %get-tuple-element.25), channel_id=1, source_target_pairs={{1,0},{2,1},{3,2},{0,3},{5,4},{6,5},{7,6},{4,7},{9,8},{10,9},{11,1... | collective-permute-start | bytes 1105928 | tf_op jit(solution)/shard_map/ppermute | solution.py:99
  122.7 16.1 %collective-permute-start.7 = (bf16[640,288]{0,1:T(8,128)(2,1)}, bf16[640,288]{0,1:T(8,128)(2,1)}, u32[]{:S(2)}, u32[]{:S(2)}) collective-permute-start(bf16[640,288]{0,1:T(8,128)(2,1)} %collective-permute-done.6), channel_id=1, source_target_pairs={{0,1},{1,2},{2,3},{3,0},{4,5},{5,6},{6,7},{7,4},{8,9},{9,10},{10,1... | collective-permute-start | bytes 1105928 | tf_op jit(solution)/shard_map/ppermute | solution.py:94
  129.4 15.4 %collective-permute-start.5 = (bf16[640,288]{0,1:T(8,128)(2,1)}, bf16[640,288]{0,1:T(8,128)(2,1)}, u32[]{:S(2)}, u32[]{:S(2)}) collective-permute-start(bf16[640,288]{0,1:T(8,128)(2,1)} %get-tuple-element.51), channel_id=1, source_target_pairs={{1,0},{2,1},{3,2},{0,3},{5,4},{6,5},{7,6},{4,7},{9,8},{10,9},{11,1... | collective-permute-start | bytes 1105928 | tf_op jit(solution)/shard_map/ppermute | solution.py:99
  131.5 13.2 %collective-permute-start.4 = (bf16[640,288]{0,1:T(8,128)(2,1)}, bf16[640,288]{0,1:T(8,128)(2,1)}, u32[]{:S(2)}, u32[]{:S(2)}) collective-permute-start(bf16[640,288]{0,1:T(8,128)(2,1)} %collective-permute-done.3), channel_id=1, source_target_pairs={{0,1},{1,2},{2,3},{3,0},{4,5},{5,6},{6,7},{7,4},{8,9},{9,10},{10,1... | collective-permute-start | bytes 1105928 | tf_op jit(solution)/shard_map/ppermute | solution.py:94
  160.9 4.3 copy-start.56
  170.2 106.4 %reduce-scatter.11.cloned.1.call-start = ((), (), s32[]{:S(2)}) async-start(), calls=%async_computation.9 | async-start | bytes 1843200 | tf_op jit(solution)/shard_map/reduce_scatter | solution.py:113
  175.9 29.3 %copy-start.9 = (f32[640,576]{0,1:T(8,128)S(1)}, f32[640,576]{0,1:T(8,128)}, u32[]{:S(2)}) copy-start(f32[640,576]{0,1:T(8,128)} %copy-done.8) | copy-start | bytes 4423684
  175.9 124.8 %reduce-scatter.19.cloned.1.call-start = ((), (), s32[]{:S(2)}) async-start(), calls=%async_computation.13 | async-start | bytes 995328 | tf_op jit(solution)/shard_map/reduce_scatter | solution.py:326
  207.0 272.2 %copy-start.11 = (f32[640,288]{0,1:T(8,128)}, f32[640,288]{0,1:T(8,128)S(1)}, u32[]{:S(2)}) copy-start(f32[640,288]{0,1:T(8,128)S(1)} %get-tuple-element.30) | copy-start | bytes 2211844
  207.0 8.9 %collective-permute-start.9 = (bf16[640,288]{0,1:T(8,128)(2,1)S(1)}, bf16[640,288]{0,1:T(8,128)(2,1)S(1)}, u32[]{:S(2)}, u32[]{:S(2)}) collective-permute-start(bf16[640,288]{0,1:T(8,128)(2,1)S(1)} %get-tuple-element.29), channel_id=1, source_target_pairs={{0,1},{1,2},{2,3},{3,0},{4,5},{5,6},{6,7},{7,4},{8,9},{9,10},{10,1... | collective-permute-start | bytes 1105928 | tf_op jit(solution)/shard_map/ppermute | solution.py:94
  207.1 10.2 %collective-permute-start.11 = (bf16[640,288]{0,1:T(8,128)(2,1)S(1)}, bf16[640,288]{0,1:T(8,128)(2,1)S(1)}, u32[]{:S(2)}, u32[]{:S(2)}) collective-permute-start(bf16[640,288]{0,1:T(8,128)(2,1)S(1)} %get-tuple-element.29), channel_id=1, source_target_pairs={{1,0},{2,1},{3,2},{0,3},{5,4},{6,5},{7,6},{4,7},{9,8},{10,9},{11,1... | collective-permute-start | bytes 1105928 | tf_op jit(solution)/shard_map/ppermute | solution.py:99
  215.9 14.2 %collective-permute-start.10 = (bf16[640,288]{0,1:T(8,128)(2,1)S(1)}, bf16[640,288]{0,1:T(8,128)(2,1)S(1)}, u32[]{:S(2)}, u32[]{:S(2)}) collective-permute-start(bf16[640,288]{0,1:T(8,128)(2,1)S(1)} %collective-permute-done.9), channel_id=1, source_target_pairs={{0,1},{1,2},{2,3},{3,0},{4,5},{5,6},{6,7},{7,4},{8,9},{9,10},{10,1... | collective-permute-start | bytes 1105928 | tf_op jit(solution)/shard_map/ppermute | solution.py:94
  238.2 135.8 %reduce-scatter.23.cloned.1.call-start = ((), (), s32[]{:S(2)}) async-start(), calls=%async_computation.15 | async-start | bytes 2985984 | tf_op jit(solution)/shard_map/reduce_scatter | solution.py:328
  244.5 202.7 %reduce-scatter.21.cloned.1.call-start = ((), (), s32[]{:S(2)}) async-start(), calls=%async_computation.14 | async-start | bytes 2985984 | tf_op jit(solution)/shard_map/reduce_scatter | solution.py:327
  250.4 226.1 %reduce-scatter.15.cloned.1.call-start = ((), (), s32[]{:S(2)}) async-start(), calls=%async_computation.11 | async-start | bytes 1843200 | tf_op jit(solution)/shard_map/reduce_scatter | solution.py:113
  252.9 6.9 %slice-start = ((s8[6553600]{0:T(1024)(128)(4,1)}), s8[4194304]{0:T(1024)(128)(4,1)S(1)}, s32[]{:S(2)}) async-start(s8[6553600]{0:T(1024)(128)(4,1)} %bitcast.132), calls=%async_computation.16 | async-start | bytes 8388608
  253.0 6.9 %slice-start.1 = ((s8[6553600]{0:T(1024)(128)(4,1)}), s8[2359296]{0:T(1024)(128)(4,1)S(1)}, s32[]{:S(2)}) async-start(s8[6553600]{0:T(1024)(128)(4,1)} %bitcast.132), calls=%async_computation.17 | async-start | bytes 4718592
  259.9 4.0 copy-start.21
  270.8 280.9 %reduce-scatter.17.cloned.1.call-start = ((), (), s32[]{:S(2)}) async-start(), calls=%async_computation.12 | async-start | bytes 2985984 | tf_op jit(solution)/shard_map/reduce_scatter | solution.py:325
  276.6 4.0 copy-start.23
  276.6 4.0 copy-start.25
  276.6 4.0 copy-start.29
  302.3 177.0 %copy-start.15 = (bf16[640,288]{0,1:T(8,128)(2,1)S(1)}, bf16[640,288]{0,1:T(8,128)(2,1)}, u32[]{:S(2)}) copy-start(bf16[640,288]{0,1:T(8,128)(2,1)} %reduce-scatter.9.cloned.1.call-done) | copy-start | bytes 1105924
  449.0 30.4 %copy-start.10 = (bf16[640,288]{0,1:T(8,128)(2,1)S(1)}, bf16[640,288]{0,1:T(8,128)(2,1)}, u32[]{:S(2)}) copy-start(bf16[640,288]{0,1:T(8,128)(2,1)} %reduce-scatter.13.cloned.1.call-done) | copy-start | bytes 1105924
  483.1 48.5 %copy-start.44 = (s32[32]{0:T(128)S(1)}, s32[32]{0:T(128)}, u32[]{:S(2)}) copy-start(s32[32]{0:T(128)} %param.21) | copy-start | bytes 388
  515.2 20.5 %copy-start.12 = (f32[640,288]{0,1:T(8,128)S(1)}, f32[640,288]{0,1:T(8,128)}, u32[]{:S(2)}) copy-start(f32[640,288]{0,1:T(8,128)} %copy-done.11) | copy-start | bytes 2211844
  515.2 20.4 %copy-start.42 = (s32[1024]{0:T(1024)S(1)}, s32[1024]{0:T(1024)}, u32[]{:S(2)}) copy-start(s32[1024]{0:T(1024)} %copy-done.40) | copy-start | bytes 12292
  535.6 17.9 %copy-start.1 = (bf16[1152,1152]{1,0:T(8,128)(2,1)S(1)}, bf16[1152,1152]{1,0:T(8,128)(2,1)}, u32[]{:S(2)}) copy-start(bf16[1152,1152]{1,0:T(8,128)(2,1)} %param.32) | copy-start | bytes 7962628
  (32 other events, 71.8 us)
Sparse Core Ops, SparseCore 0:
  90.4 27.8 reduce-scatter.8
  170.3 27.2 reduce-scatter.12
  200.2 31.4 reduce-scatter.10
  238.3 62.2 reduce-scatter.18
  304.6 69.3 reduce-scatter.22
  377.5 69.6 reduce-scatter.20
  449.9 26.5 reduce-scatter.14
  480.2 71.4 reduce-scatter.16
